TPU v7x, 32 devices: a whole 2x2x4 slice. The times are simulated.
32 devices in a mesh: dp: 4 (over x, core), seq: 8 (over z, y).
Axes of the slice: x: 2, y: 2, z: 4, core: 2. Of those that a mesh axis runs over, the one named last changes fastest.
Arguments:
- tokens: bfloat16 [32768, 1152], P(('dp', 'seq')), may hold values from -6 to 6
- condition: bfloat16 [128, 1152], P('dp'), may hold values from -6 to 6
- lengths: int32 [128], P(('dp', 'seq')), may hold values from 1 to 256, 22937 in all
- kept_index: int32 [128, 256], P(('dp', 'seq')), may hold values from 0 to 255, each once within a row
- heads_weight: bfloat16 [1152, 3456], P('seq'), may hold values from -0.1875 to 0.1875
- heads_bias: bfloat16 [2304], replicated, may hold values from -1.5 to 1.5
- merge_weight: bfloat16 [1152, 1152], P('seq'), may hold values from -1.5 to 1.5
- merge_bias: bfloat16 [1152], replicated, may hold values from -4 to 4
- up_weight: bfloat16 [1152, 4608], P('seq'), may hold values from -0.1875 to 0.1875
- up_bias: bfloat16 [4608], replicated, may hold values from -4 to 4
- down_weight: bfloat16 [1152, 4608], P('seq'), may hold values from -0.1875 to 0.1875
- down_bias: bfloat16 [1152], replicated, may hold values from -4 to 4
- modulate_weight: bfloat16 [1152, 6912], P('seq'), may hold values from -0.1875 to 0.1875
- modulate_bias: bfloat16 [6912], replicated, may hold values from -4 to 4
- relative_table: bfloat16 [16, 961], replicated, may hold values from -6 to 6
- cotangent: bfloat16 [32768, 1152], P(('dp', 'seq')), may hold values from -6 to 6
Outputs:
- output: bfloat16 [32768, 1152], P(('dp', 'seq'))
- tokens_grad: float32 [32768, 1152], P(('dp', 'seq'))
- heads_weight_grad: float32 [1152, 3456], P('seq')
- merge_weight_grad: float32 [1152, 1152], P('seq')
- up_weight_grad: float32 [1152, 4608], P('seq')
- down_weight_grad: float32 [1152, 4608], P('seq')
- modulate_weight_grad: float32 [1152, 6912], P('seq')
- heads_bias_grad: float32 [2304], replicated
- merge_bias_grad: float32 [1152], replicated
- up_bias_grad: float32 [4608], replicated
- down_bias_grad: float32 [1152], replicated
- modulate_bias_grad: float32 [6912], replicated
- relative_table_grad: float32 [16, 961], replicated
Inputs may be any that keep to these rules, and one draw needn't show every extreme that they name: The first lengths[s] slots of sample s hold its kept tokens, the rest are empty. Each sample's row is a permutation of the 256 patch positions; slot r's patch lies at row kept_index // 16, column kept_index % 16.
All inputs are finite; a program needn't handle non-finite values. No bound on the sum of `lengths` on one device may be relied on, other than what follows from the above.
Results may differ from a plain program's by a relative error of at most 0.019.
Values may be sent and summed in bfloat16 or wider, within the bound.
No kernel may reach another device: no remote copies, remote signals or barrier semaphores. Data moves between devices by JAX's collectives and lax.ppermute only.
A program may use at most 320 MiB of HBM per device.

v0:
```python
from functools import partial
import math
import jax
import jax.numpy as jnp
from jax import lax
from jax.sharding import PartitionSpec as P

D = 1152
HEADS = 16
HEAD = 72
FF = 4608
SIDE = 16
MICRO = 2
SAMP_DEV = 4
GRID = 256
epsilon = 1e-06


def layer_norm(values):
    center = values - jnp.mean(values, axis=-1, keepdims=True)
    spread = jnp.mean(center * center, axis=-1, keepdims=True)
    return center * lax.rsqrt(spread + epsilon)


def modulated(values, scales, shifts):
    return layer_norm(values) * (1.0 + scales) + shifts


def gelu_tanh(values):
    return jax.nn.gelu(values, approximate=True)


def fold_rows(left, portion):
    return jnp.dot(left, portion, preferred_element_type=jnp.float32)


def right_transposed(left, portion):
    return lax.dot_general(
        left, portion, (((1,), (1,)), ((), ())), preferred_element_type=jnp.float32
    )


def column_outer(left, right):
    return lax.dot_general(
        left, right, (((0,), (0,)), ((), ())), preferred_element_type=jnp.float32
    )


def relative_index(positions):
    row_place = positions // SIDE
    col_place = positions % SIDE
    row_gap = row_place[..., :, None] - row_place[..., None, :] + (SIDE - 1)
    col_gap = col_place[..., :, None] - col_place[..., None, :] + (SIDE - 1)
    return row_gap * (2 * SIDE - 1) + col_gap


def slot_onehot(index_pair):
    return (index_pair[..., :, None] == jnp.arange(GRID)[None, None, :]).astype(jnp.bfloat16)


def pair_scores(packed, lens_pair, index_pair, position_bias):
    parts = packed.reshape(2, GRID, 3, HEADS, HEAD)
    queries = parts[:, :, 0]
    key_part = parts[:, :, 1]
    value_part = parts[:, :, 2]
    scaling = 1.0 / math.sqrt(HEAD)
    onehot = slot_onehot(index_pair)
    rows_placed = jnp.einsum(
        "srp,hpq->hsrq", onehot, position_bias, preferred_element_type=jnp.float32
    ).astype(jnp.bfloat16)
    bias_pair = jnp.einsum(
        "hsrq,skq->hsrk", rows_placed, onehot, preferred_element_type=jnp.float32
    )
    scores = (
        jnp.einsum("sqhe,skhe->hsqk", queries, key_part, preferred_element_type=jnp.float32)
        * scaling
    )
    scores = scores + bias_pair
    living = jnp.arange(GRID)[None, :] < lens_pair[:, None]
    scores = jnp.where(living[None, :, None, :], scores, -1e30)
    return (scores, queries, key_part, value_part, onehot)


def attend_pair(arguments, position_bias):
    packed, lens_pair, index_pair = arguments
    scores, queries, key_part, value_part, onehot = pair_scores(
        packed, lens_pair, index_pair, position_bias
    )
    peak = jnp.max(scores, axis=-1, keepdims=True)
    expo = jnp.exp(scores - peak)
    mass = jnp.sum(expo, axis=-1, keepdims=True)
    probs_low = (expo / mass).astype(jnp.bfloat16)
    mixed = jnp.einsum("hsqk,skhe->sqhe", probs_low, value_part, preferred_element_type=jnp.float32)
    return (mixed.astype(jnp.bfloat16).reshape(2 * GRID, D), (peak + jnp.log(mass))[..., 0])


def attend_pair_back(arguments, position_bias):
    packed, lens_pair, index_pair, logsum, grad_mixed = arguments
    scores, queries, key_part, value_part, onehot = pair_scores(
        packed, lens_pair, index_pair, position_bias
    )
    probs = jnp.exp(scores - logsum[..., None])
    grad_mixed = grad_mixed.reshape(2, GRID, HEADS, HEAD)
    grad_probs = jnp.einsum(
        "sqhe,skhe->hsqk", grad_mixed, value_part, preferred_element_type=jnp.float32
    )
    inner = jnp.sum(probs * grad_probs, axis=-1, keepdims=True)
    grad_scores = (probs * (grad_probs - inner)).astype(jnp.bfloat16)
    scaling = 1.0 / math.sqrt(HEAD)
    grad_query = (
        jnp.einsum("hsqk,skhe->sqhe", grad_scores, key_part, preferred_element_type=jnp.float32)
        * scaling
    )
    grad_key = (
        jnp.einsum("hsqk,sqhe->skhe", grad_scores, queries, preferred_element_type=jnp.float32)
        * scaling
    )
    grad_value = jnp.einsum(
        "hsqk,sqhe->skhe",
        probs.astype(jnp.bfloat16),
        grad_mixed,
        preferred_element_type=jnp.float32,
    )
    stacked = (
        jnp.stack([grad_query, grad_key, grad_value], axis=2)
        .astype(jnp.bfloat16)
        .reshape(2 * GRID, 3 * D)
    )
    rows_back = jnp.einsum(
        "hsrk,srp->hspk", grad_scores, onehot, preferred_element_type=jnp.float32
    ).astype(jnp.bfloat16)
    placed_grad = jnp.einsum("hspk,skq->hpq", rows_back, onehot, preferred_element_type=jnp.float32)
    return (stacked, placed_grad)


def offsets_table(placed_grad):
    spots = jnp.arange(SIDE)
    reach = jnp.arange(2 * SIDE - 1)
    gaps = (
        spots[:, None, None] - spots[None, :, None] + (SIDE - 1) == reach[None, None, :]
    ).astype(jnp.float32)
    grid_grad = placed_grad.reshape(HEADS, SIDE, SIDE, SIDE, SIDE)
    by_rows = jnp.einsum("hwxyz,wya->haxz", grid_grad, gaps, precision=lax.Precision.HIGHEST)
    return jnp.einsum("haxz,xzb->hab", by_rows, gaps, precision=lax.Precision.HIGHEST).reshape(
        HEADS, (2 * SIDE - 1) ** 2
    )


def local(
    tokens,
    condition,
    lengths,
    kept_index,
    heads_weight,
    heads_bias,
    merge_weight,
    merge_bias,
    up_weight,
    up_bias,
    down_weight,
    down_bias,
    modulate_weight,
    modulate_bias,
    relative_table,
    cotangent,
):
    position = lax.axis_index("seq")
    position_bias = jnp.take(relative_table, relative_index(jnp.arange(GRID)), axis=1)
    own_cond = lax.dynamic_slice_in_dim(condition, position * SAMP_DEV, SAMP_DEV, 0)
    own_silu = jax.nn.silu(own_cond.astype(jnp.float32)).astype(jnp.bfloat16)
    modulation = fold_rows(own_silu, lax.all_gather(modulate_weight, "seq", axis=0, tiled=True))
    modulation = (modulation + modulate_bias.astype(jnp.float32)).reshape(SAMP_DEV, 1, 6, D)
    full_bias = jnp.concatenate(
        [heads_bias[:D], jnp.zeros((D,), jnp.bfloat16), heads_bias[D:]]
    ).astype(jnp.float32)
    parts_count = MICRO
    samples = SAMP_DEV // parts_count
    rows = samples * GRID
    pairs = samples // 2
    kept = {
        "out": [],
        "tgrad": [],
        "mgrad": [],
        "hone": [],
        "gpack": [],
        "attn": [],
        "gbranch": [],
        "htwo": [],
        "gup": [],
        "gmlp": [],
        "act": [],
    }
    placed_total = jnp.zeros((HEADS, GRID, GRID), jnp.float32)
    for part in range(parts_count):
        slab = tokens[part * rows : (part + 1) * rows].astype(jnp.float32).reshape(samples, GRID, D)
        mods = modulation[part * samples : (part + 1) * samples]
        shift_one, scale_one, gate_one, shift_two, scale_two, gate_two = [
            mods[:, :, index] for index in range(6)
        ]
        lens_part = lengths[part * samples : (part + 1) * samples]
        index_part = kept_index[part * samples : (part + 1) * samples]
        living = (jnp.arange(GRID)[None, :] < lens_part[:, None])[:, :, None]
        hidden_one = modulated(slab, scale_one, shift_one).astype(jnp.bfloat16).reshape(rows, D)
        packed = (
            fold_rows(hidden_one, lax.all_gather(heads_weight, "seq", axis=0, tiled=True))
            + full_bias
        ).astype(jnp.bfloat16)
        packed_pairs = packed.reshape(pairs, 2 * GRID, 3 * D)
        lens_pairs = lens_part.reshape(pairs, 2)
        index_pairs = index_part.reshape(pairs, 2, GRID)
        attended, logsum = lax.map(
            partial(attend_pair, position_bias=position_bias),
            (packed_pairs, lens_pairs, index_pairs),
        )
        attended = attended.reshape(rows, D)
        branch = fold_rows(
            attended, lax.all_gather(merge_weight, "seq", axis=0, tiled=True)
        ) + merge_bias.astype(jnp.float32)
        branch = branch.reshape(samples, GRID, D)
        middle = slab + gate_one * branch
        hidden_two = modulated(middle, scale_two, shift_two).astype(jnp.bfloat16).reshape(rows, D)
        up_value = fold_rows(
            hidden_two, lax.all_gather(up_weight, "seq", axis=0, tiled=True)
        ) + up_bias.astype(jnp.float32)
        activated = gelu_tanh(up_value).astype(jnp.bfloat16)
        mlp_out = right_transposed(
            activated, lax.all_gather(down_weight, "seq", axis=0, tiled=True)
        )
        mlp_out = (mlp_out + down_bias.astype(jnp.float32)).reshape(samples, GRID, D)
        final = jnp.where(living, middle + gate_two * mlp_out, 0.0)
        kept["out"].append(final.astype(jnp.bfloat16).reshape(rows, D))
        grad_final = jnp.where(
            living,
            cotangent[part * rows : (part + 1) * rows]
            .astype(jnp.float32)
            .reshape(samples, GRID, D),
            0.0,
        )
        gate_two_grad = jnp.sum(grad_final * mlp_out, axis=1, keepdims=True)
        grad_mlp = (gate_two * grad_final).astype(jnp.bfloat16).reshape(rows, D)
        grad_act = fold_rows(grad_mlp, lax.all_gather(down_weight, "seq", axis=0, tiled=True))
        grad_up = jax.vjp(gelu_tanh, up_value)[1](grad_act)[0].astype(jnp.bfloat16)
        grad_hidden_two = right_transposed(
            grad_up, lax.all_gather(up_weight, "seq", axis=0, tiled=True)
        )
        middle_ln, scale_two_grad, shift_two_grad = jax.vjp(
            modulated, middle, scale_two, shift_two
        )[1](grad_hidden_two.reshape(samples, GRID, D))
        grad_middle = grad_final + middle_ln
        gate_one_grad = jnp.sum(grad_middle * branch, axis=1, keepdims=True)
        grad_branch = (gate_one * grad_middle).astype(jnp.bfloat16).reshape(rows, D)
        grad_attended = right_transposed(
            grad_branch, lax.all_gather(merge_weight, "seq", axis=0, tiled=True)
        ).astype(jnp.bfloat16)
        grad_packed, placed_parts = lax.map(
            partial(attend_pair_back, position_bias=position_bias),
            (
                packed_pairs,
                lens_pairs,
                index_pairs,
                logsum,
                grad_attended.reshape(pairs, 2 * GRID, D),
            ),
        )
        grad_packed = grad_packed.reshape(rows, 3 * D)
        placed_total = placed_total + jnp.sum(placed_parts, axis=0)
        grad_hidden_one = right_transposed(
            grad_packed, lax.all_gather(heads_weight, "seq", axis=0, tiled=True)
        )
        slab_ln, scale_one_grad, shift_one_grad = jax.vjp(modulated, slab, scale_one, shift_one)[1](
            grad_hidden_one.reshape(samples, GRID, D)
        )
        kept["tgrad"].append((grad_middle + slab_ln).reshape(rows, D))
        kept["mgrad"].append(
            jnp.concatenate(
                [
                    shift_one_grad,
                    scale_one_grad,
                    gate_one_grad,
                    shift_two_grad,
                    scale_two_grad,
                    gate_two_grad,
                ],
                axis=-1,
            ).reshape(samples, 6 * D)
        )
        kept["hone"].append(hidden_one)
        kept["gpack"].append(grad_packed)
        kept["attn"].append(attended)
        kept["gbranch"].append(grad_branch)
        kept["htwo"].append(hidden_two)
        kept["gup"].append(grad_up)
        kept["gmlp"].append(grad_mlp)
        kept["act"].append(activated)
    table_grad = offsets_table(placed_total)
    joined = {name: jnp.concatenate(items, axis=0) for name, items in kept.items()}
    mod_grad = joined["mgrad"].astype(jnp.bfloat16)
    pieces = [
        column_outer(joined["hone"], joined["gpack"]),
        column_outer(joined["attn"], joined["gbranch"]),
        column_outer(joined["htwo"], joined["gup"]),
        column_outer(joined["gmlp"], joined["act"]),
        column_outer(own_silu, mod_grad),
    ]
    summed = lax.psum_scatter(
        jnp.concatenate(pieces, axis=1).astype(jnp.bfloat16), "seq", scatter_dimension=0, tiled=True
    )
    share = lax.psum_scatter(summed, "dp", scatter_dimension=0, tiled=True).astype(jnp.float32)
    replicated = lax.all_gather(share.astype(jnp.bfloat16), "dp", axis=0, tiled=True).astype(
        share.dtype
    )
    packed_sums = jnp.sum(joined["gpack"], axis=0, dtype=jnp.float32)
    heads_part = jnp.concatenate([packed_sums[:D], packed_sums[2 * D :]])
    merge_part = jnp.sum(joined["gbranch"], axis=0, dtype=jnp.float32)
    up_part = jnp.sum(joined["gup"], axis=0, dtype=jnp.float32)
    down_part = jnp.sum(joined["gmlp"], axis=0, dtype=jnp.float32)
    modulate_part = jnp.sum(mod_grad, axis=0, dtype=jnp.float32)
    heads_total, merge_total, up_total, down_total, modulate_total, table_total = lax.psum(
        (heads_part, merge_part, up_part, down_part, modulate_part, table_grad), ("dp", "seq")
    )
    edges = [0, 3 * D, 4 * D, 4 * D + FF, 4 * D + 2 * FF, 10 * D + 2 * FF]
    return (
        joined["out"],
        joined["tgrad"],
        replicated[:, edges[0] : edges[1]],
        replicated[:, edges[1] : edges[2]],
        replicated[:, edges[2] : edges[3]],
        replicated[:, edges[3] : edges[4]],
        replicated[:, edges[4] : edges[5]],
        heads_total,
        merge_total,
        up_total,
        down_total,
        modulate_total,
        table_total,
    )


def solution(mesh):
    in_specs = (
        P(("dp", "seq"), None),
        P("dp", None),
        P(("dp", "seq")),
        P(("dp", "seq"), None),
        P("seq", None),
        P(),
        P("seq", None),
        P(),
        P("seq", None),
        P(),
        P("seq", None),
        P(),
        P("seq", None),
        P(),
        P(),
        P(("dp", "seq"), None),
    )
    out_specs = (
        P(("dp", "seq"), None),
        P(("dp", "seq"), None),
        P("seq", None),
        P("seq", None),
        P("seq", None),
        P("seq", None),
        P("seq", None),
        P(),
        P(),
        P(),
        P(),
        P(),
        P(),
    )
    return jax.shard_map(local, mesh=mesh, in_specs=in_specs, out_specs=out_specs, check_vma=False)
```

profile of v0, /device:TPU:8, one launch (start us, length us, event | category | flops | bytes accessed | tf_op | source)
XLA Modules:
  0.0 2067.6 jit_solution(3447131822799105786)
XLA Ops:
  21.8 4.3 slice_convert_fusion.1
  26.2 227.7 %gather_fusion = bf16[65536,16]{1,0:T(8,128)(2,1)} fusion(bf16[16,961]{0,1:T(8,128)(2,1)S(1)} %copy.147, s32[65536]{0:T(1024)S(1)} %broadcast_clamp_fusion), kind=kCustom, calls=%fused_computation | custom fusion | bytes 4456448 | tf_op jit(solution)/shard_map/jit(_take)/gather | solution.py:168
  253.8 16.7 copy.148
  270.6 5.1 convert_bitcast_fusion
  275.6 3.4 convert_bitcast_fusion.1
  279.7 7.9 convolution_add_fusion
  292.3 54.5 %all-gather.10.cloned.1.call-done = bf16[1152,3456]{1,0:T(8,128)(2,1)} async-done(((bf16[144,3456]{1,0:T(8,128)(2,1)}), bf16[1152,3456]{1,0:T(8,128)(2,1)}) %all-gather.10.cloned.1.call-update) | async-done | bytes 7962640 | tf_op jit(solution)/shard_map/all_gather | solution.py:205
  346.7 9.5 add_convert_fusion.1
  356.3 5.8 copy.143
  362.1 8.3 reshape.859
  370.4 15.9 fusion.217
  399.5 4.5 all-gather.12.cloned.1.call-done
  404.0 6.8 fusion.212
  411.4 11.2 add_convert_fusion
  422.6 5.7 copy.152
  428.3 8.3 reshape.861
  436.7 3.9 fusion.218
  453.6 4.2 fusion.214
  467.8 87.5 %all-gather.14.cloned.1.call-done = bf16[1152,4608]{1,0:T(8,128)(2,1)} async-done(((bf16[144,4608]{1,0:T(8,128)(2,1)}), bf16[1152,4608]{1,0:T(8,128)(2,1)}) %all-gather.14.cloned.1.call-update) | async-done | bytes 10616848 | tf_op jit(solution)/shard_map/all_gather | solution.py:223
  555.3 11.7 fusion.231
  566.9 8.9 fusion.230
  575.8 132.2 %all-gather.16.cloned.1.call-done = bf16[1152,4608]{1,0:T(8,128)(2,1)} async-done(((bf16[144,4608]{1,0:T(8,128)(2,1)}), bf16[1152,4608]{1,0:T(8,128)(2,1)}) %all-gather.16.cloned.1.call-update) | async-done | bytes 10616848 | tf_op jit(solution)/shard_map/all_gather | solution.py:227
  708.0 11.6 fusion.232
  719.6 24.2 %fusion.11 = (bf16[512,4608]{1,0:T(8,128)(2,1)}, bf16[512,4608]{1,0:T(8,128)(2,1)}, bf16[512,4608]{1,0:T(8,128)(2,1)}, bf16[512,4608]{1,0:T(8,128)(2,1)}) fusion(f32[512,4608]{1,0:T(8,128)} %fusion.230, f32[4608]{0:T(1024)S(1)} %copy-done.104, f32[512,4608]{1,0:T(8,128)} %fusion.231, f32[512,4608]{1,0:T(8,128)} %fusion.232, ...), kind=kOutput, calls=%fused_computation.21 | convolution fusion | flops 5544345600 | bytes 59000832 | tf_op jit(solution)/shard_map/dot_general | solution.py:34
  743.8 12.7 multiply_reduce_fusion.11
  757.2 13.2 multiply_reduce_fusion.9
  771.0 14.4 fusion.210
  785.5 13.1 fusion.211
  799.8 3.8 fusion.71
  807.9 2.9 reshape.867
  810.9 5.3 multiply_reduce_fusion.1
  819.1 3.6 multiply_bitcast_fusion.2
  825.6 3.6 copy.181
  832.8 4.8 convolution_convert_fusion.4
  842.9 3.7 reshape.873
  847.4 6.1 multiply_reduce_fusion
  854.0 4.0 multiply_convert_fusion.2
  858.0 3.7 multiply_bitcast_fusion
  864.9 5.5 copy.182
  874.3 5.2 copy.183
  883.6 8.8 multiply_reduce_fusion.10
  899.8 10.3 multiply_reduce_fusion.8
  910.2 4.8 multiply_reduce_fusion.4
  916.6 10.9 fusion.4
  927.5 3.5 constant_dynamic-update-slice_fusion.14
  931.0 17.3 fusion.3
  948.4 16.6 fusion.2
  965.1 4.2 multiply_reduce_fusion.6
  971.1 3.7 multiply_reduce_fusion.5
  975.5 8.7 fusion.1
  984.2 748.7 %reduce-scatter.4.cloned.1.call-done = bf16[144,20736]{1,0:T(8,128)(2,1)} async-done(((bf16[1152,20736]{1,0:T(8,128)(2,1)}), bf16[144,20736]{1,0:T(8,128)(2,1)}) %reduce-scatter.4.cloned.1.call-update) | async-done | bytes 5971984 | tf_op jit(solution)/shard_map/reduce_scatter | solution.py:305
  1732.9 62.0 %fusion = bf16[40,20736]{1,0:T(8,128)(2,1)} fusion(bf16[144,20736]{1,0:T(8,128)(2,1)} %reduce-scatter.4.cloned.1.call-done), kind=kCustom, calls=%all-reduce-scatter | all-reduce-scatter fusion | flops 3317761 | bytes 7631360
  1800.4 17.0 concatenate.72
  1817.4 3.1 dynamic-slice_bitcast_fusion
  1820.6 6.8 fusion.32
  1827.4 8.1 bitcast_add_fusion.2
  1835.4 19.8 add.547
  1855.2 33.3 %fusion.185 = f32[31,16,16,16,1]{0,3,2,4,1:T(8,128)} fusion(f32[16,16,16,16,16]{4,3,2,1,0:T(8,128)} %add.547, s32[16,16]{1,0:T(8,128)S(1)} %subtract_add_fusion), kind=kOutput, calls=%fused_computation.258 | convolution fusion | flops 390078208 | bytes 4703232 | tf_op jit(solution)/shard_map/hwxyz,wya->haxz/dot_general | solution.py:143
  1888.6 4.1 fusion.151
  1896.0 4.2 convert_reduce_fusion.1
  1911.9 4.3 convert_reduce_fusion
  1916.3 10.3 reshape.899
  1926.6 5.7 fusion.216
  1938.7 113.8 %all-reduce.5.cloned.1.call-done = (f32[2304]{0:T(1024)}, f32[1152]{0:T(1024)}, f32[4608]{0:T(1024)}, f32[1152]{0:T(1024)}, f32[6912]{0:T(1024)}, /*index=5*/f32[16,961]{1,0:T(8,128)}) async-done(((f32[2304]{0:T(1024)}, f32[1152]{0:T(1024)}, f32[4608]{0:T(1024)}, f32[1152]{0:T(1024)}, f32[6912]{0:T(1024)}, /*index=5*/f32[16,961]{1,0:T(8,128)}), (f32[2304]{0:T(1024)}, f32[1152]{0:T(1024)}, f32[4608]{0:T(1024)}, ...) | async-done | bytes 126032 | tf_op jit(solution)/shard_map/psum | solution.py:318
  (480 shorter events, 135.2 us)
Async XLA Ops:
  7.2 272.5 %all-gather.8.cloned.1.call-start = ((), (), s32[]{:S(2)}) async-start(), calls=%async_computation.1 | async-start | bytes 17915904 | tf_op jit(solution)/shard_map/all_gather | solution.py:171
  7.9 338.8 %all-gather.10.cloned.1.call-start = ((), (), s32[]{:S(2)}) async-start(), calls=%async_computation.2 | async-start | bytes 8957952 | tf_op jit(solution)/shard_map/all_gather | solution.py:205
  8.7 395.3 %all-gather.12.cloned.1.call-start = ((), (), s32[]{:S(2)}) async-start(), calls=%async_computation.3 | async-start | bytes 2985984 | tf_op jit(solution)/shard_map/all_gather | solution.py:217
  9.4 545.9 %all-gather.14.cloned.1.call-start = ((), (), s32[]{:S(2)}) async-start(), calls=%async_computation.4 | async-start | bytes 11943936 | tf_op jit(solution)/shard_map/all_gather | solution.py:223
  10.0 698.0 %all-gather.16.cloned.1.call-start = ((), (), s32[]{:S(2)}) async-start(), calls=%async_computation.5 | async-start | bytes 11943936 | tf_op jit(solution)/shard_map/all_gather | solution.py:227
  10.6 1722.4 %reduce-scatter.4.cloned.1.call-start = ((), (), s32[]{:S(2)}) async-start(), calls=%async_computation.6 | async-start | bytes 53747712 | tf_op jit(solution)/shard_map/reduce_scatter | solution.py:305
  13.3 6.3 copy-start.150
  13.4 6.8 copy-start.151
  13.4 7.4 copy-start.128
  13.4 7.4 copy-start.129
  13.4 8.1 copy-start.127
  13.4 8.1 copy-start.100
  17.2 253.4 %copy-start.135 = (s32[2,256]{1,0:T(2,128)}, s32[2,256]{1,0:T(2,128)S(1)}, u32[]{:S(2)}) copy-start(s32[2,256]{1,0:T(2,128)S(1)} %get-tuple-element.193) | copy-start | bytes 6148
  17.2 370.5 %copy-start.98 = (s32[2,256]{1,0:T(2,128)}, s32[2,256]{1,0:T(2,128)S(1)}, u32[]{:S(2)}) copy-start(s32[2,256]{1,0:T(2,128)S(1)} %get-tuple-element.192) | copy-start | bytes 6148
  292.3 64.0 %copy-start.63 = (bf16[512,1152]{1,0:T(8,128)(2,1)}, bf16[512,1152]{1,0:T(8,128)(2,1)S(1)}, u32[]{:S(2)}) copy-start(bf16[512,1152]{1,0:T(8,128)(2,1)S(1)} %fusion.98) | copy-start | bytes 3538948
  386.3 7.4 copy-start.35
  397.3 6.7 copy-start.103
  398.8 12.0 copy-start.54
  399.5 11.3 copy-start.70
  440.6 7.9 copy-start.37
  461.2 309.8 %copy-start.74 = (f32[2,1152]{1,0:T(2,128)}, f32[2,1152]{1,0:T(2,128)S(1)}, u32[]{:S(2)}) copy-start(f32[2,1152]{1,0:T(2,128)S(1)} %get-tuple-element.239) | copy-start | bytes 27652
  464.0 321.5 %copy-start.81 = (f32[2,1152]{1,0:T(2,128)}, f32[2,1152]{1,0:T(2,128)S(1)}, u32[]{:S(2)}) copy-start(f32[2,1152]{1,0:T(2,128)S(1)} %get-tuple-element.235) | copy-start | bytes 27652
  555.3 11.7 copy-start.66
  555.3 11.7 copy-start.155
  708.0 11.6 copy-start.5
  708.0 11.6 copy-start.104
  757.2 13.2 copy-start.110
  757.2 13.8 copy-start.88
  757.2 13.8 copy-start.108
  757.2 13.8 copy-start.149
  771.0 14.5 copy-start.10
  771.0 14.5 copy-start.11
  771.0 14.5 copy-start.106
  771.0 14.5 copy-start.147
  785.5 14.2 copy-start.71
  847.4 6.1 slice-start.2
  847.4 6.6 slice-start.3
  883.5 8.9 copy-start.139
  883.5 8.9 copy-start.1
  883.5 8.9 copy-start.13
  883.5 8.9 copy-start.15
  883.6 8.9 copy-start.114
  899.8 10.3 copy-start.138
  899.8 10.4 copy-start.12
  899.8 10.4 copy-start.14
  899.8 10.4 copy-start.73
  899.8 10.4 copy-start.115
  916.6 10.9 copy-start.17
  931.0 17.3 copy-start.52
  948.3 16.7 copy-start.75
  948.3 16.7 copy-start.126
  948.3 16.7 copy-start.134
  965.1 6.0 copy-start.28
  965.1 6.0 copy-start.82
  984.2 815.0 %copy-start.154 = (u32[32]{0:T(128)S(1)}, u32[32]{0:T(128)}, u32[]{:S(2)}) copy-start(u32[32]{0:T(128)} %constant.195) | copy-start | bytes 388
  984.2 932.1 %all-gather.18.cloned.1.call-start = ((), (), s32[]{:S(2)}) async-start(), calls=%async_computation.7 | async-start | bytes 8294400 | tf_op jit(solution)/shard_map/all_gather | solution.py:309
  1797.0 3.4 collective-permute-start
  1820.5 232.0 %all-reduce.5.cloned.1.call-start = ((), (), s32[]{:S(2)}) async-start(), calls=%async_computation.8 | async-start | bytes 286720 | tf_op jit(solution)/shard_map/psum | solution.py:318
  1820.6 6.8 copy-start.99
  1896.0 6.8 copy-start.43
  1896.0 6.9 copy-start.44
  1896.0 8.5 copy-start.77
  1896.0 8.5 copy-start.80
  1926.6 8.5 copy-start.4
  (107 other events, 345.6 us)
Sparse Core Ops, SparseCore 0:
  10.2 216.5 all-gather.7
  228.9 117.7 all-gather.9
  348.9 55.0 all-gather.11
  406.0 149.1 all-gather.13
  557.3 150.6 all-gather.15
  984.3 748.6 reduce-scatter.3
  1820.6 57.1 all-gather.17
  1916.3 136.0 all-reduce.4
where the time goes:
time: 2070 us
  waiting for transfers between devices  1140 us (55%)
  local copies, waits for them, and re-layouts  442 us (21%)
  matrix products  327 us (16%)
  other arithmetic  72.9 us (4%)
  blocking collectives  62 us (3%)
    reduce_scatter x1, waiting for transfers between devices, local(): lax.psum_scatter(jnp.concatenate(pieces, axis=1).astype(jnp.bfloat16), 's...  749 us
    gather x2, local copies, waits for them, and re-layouts, local(): jnp.take(relative_table, relative_index(jnp.arange(GRID)), axis=1)  244 us
    all_gather x1, waiting for transfers between devices, local(): lax.all_gather(down_weight, 'seq', axis=0, tiled=True)  132 us
    psum x1, waiting for transfers between devices, local(): lax.psum((heads_part, merge_part, up_part, down_part, modulate_part, tabl...  114 us
    dot_general x9, matrix products, fold_rows(): return jnp.dot(left, portion, preferred_element_type=jnp.float32)  96.1 us
    all_gather x1, waiting for transfers between devices, local(): lax.all_gather(up_weight, 'seq', axis=0, tiled=True)  87.5 us
    dot_general x8, matrix products, right_transposed(): lax.dot_general(left, portion, (((1,), (1,)), ((), ())), preferred_elemen...  77.3 us
    unnamed x359, local copies, waits for them, and re-layouts  65.2 us
  transfers between devices with their start and end apart: 9, of which 6 were waited for; matrix products, arithmetic and copies ran while one was open for 25% of the time, Pallas kernels for 0%

commit v1 on v0

--- a/solution.py
+++ b/solution.py
@@ -1,3 +1,4 @@
+import functools
 from functools import partial
 import math
 import jax
@@ -14,6 +15,32 @@
 SAMP_DEV = 4
 GRID = 256
 epsilon = 1e-06
+
+
+def _handle_signs(u_in, axis_no):
+    u_in = jnp.moveaxis(u_in, 0, axis_no)
+    tall = u_in.shape
+    return u_in.reshape(*tall[:axis_no], tall[axis_no] * tall[axis_no + 1], *tall[axis_no + 2 :])
+
+
+def unite_runs(arr_in, group_axis, row_dim):
+    wide_n = lax.axis_size(group_axis)
+    rack = [(m, (m + 1) % wide_n) for m in range(wide_n)]
+    block_list = [(dev, nth) for nth, dev in rack]
+    oldest, placed = ([], [])
+    for p in range(wide_n - 1):
+        if p % 2 == 0:
+            oldest.append(lax.ppermute(oldest[-1] if oldest else arr_in, group_axis, rack))
+        else:
+            item_now = lax.ppermute(placed[-1] if placed else arr_in, group_axis, block_list)
+            placed.append(item_now)
+    u_next = jnp.stack([*oldest[::-1], arr_in, *placed])
+    z_new = lax.axis_index(group_axis) - len(oldest)
+    u_next = u_next[(jnp.arange(wide_n) - z_new) % wide_n]
+    return _handle_signs(u_next, row_dim)
+
+
+_begin_corner = functools.partial(unite_runs, group_axis="seq", row_dim=0)
 
 
 def layer_norm(values):
@@ -201,10 +228,9 @@
         index_part = kept_index[part * samples : (part + 1) * samples]
         living = (jnp.arange(GRID)[None, :] < lens_part[:, None])[:, :, None]
         hidden_one = modulated(slab, scale_one, shift_one).astype(jnp.bfloat16).reshape(rows, D)
-        packed = (
-            fold_rows(hidden_one, lax.all_gather(heads_weight, "seq", axis=0, tiled=True))
-            + full_bias
-        ).astype(jnp.bfloat16)
+        packed = (fold_rows(hidden_one, _begin_corner(heads_weight)) + full_bias).astype(
+            jnp.bfloat16
+        )
         packed_pairs = packed.reshape(pairs, 2 * GRID, 3 * D)
         lens_pairs = lens_part.reshape(pairs, 2)
         index_pairs = index_part.reshape(pairs, 2, GRID)

time: 2070 us -> 2030 us (0.981)
  waiting for transfers between devices: 1140 us -> 1080 us
    ppermute x0 -> x7, waiting for transfers between devices: none -> 116 us  [the longest x4 99.4 us: unite_runs(): lax.ppermute(oldest[-1] if oldest else arr_in, group_axis, rack)]
    all_gather x1, waiting for transfers between devices: 87.5 us -> 0.01 us  [local(): lax.all_gather(up_weight, 'seq', axis=0, tiled=True)]
    all_gather x1, waiting for transfers between devices: 54.5 us -> 0.01 us  [local(): lax.all_gather(heads_weight, 'seq', axis=0, tiled=True)]
    all_gather x1, waiting for transfers between devices: 132 us -> 102 us  [local(): lax.all_gather(down_weight, 'seq', axis=0, tiled=True)]
    unnamed x359 -> x367, local copies, waits for them, and re-layouts: 65.2 us -> 75.7 us
  transfers between devices with their start and end apart: 9 -> 16, of which waited for: 6 -> 8; matrix products, arithmetic and copies ran while one was open for 25% -> 35% of each run, Pallas kernels for 0% -> 0%
where the time goes in v1:
time: 2030 us; the launch traced here: 2020 us
  waiting for transfers between devices  1080 us (53%)
  local copies, waits for them, and re-layouts  452 us (22%)
  matrix products  326 us (16%)
  other arithmetic  71.1 us (4%)
  blocking collectives  61.9 us (3%)
    reduce_scatter x1, waiting for transfers between devices, local(): lax.psum_scatter(jnp.concatenate(pieces, axis=1).astype(jnp.bfloat16), 's...  749 us
    gather x2, local copies, waits for them, and re-layouts, local(): jnp.take(relative_table, relative_index(jnp.arange(GRID)), axis=1)  244 us
    psum x1, waiting for transfers between devices, local(): lax.psum((heads_part, merge_part, up_part, down_part, modulate_part, tabl...  114 us
    all_gather x1, waiting for transfers between devices, local(): lax.all_gather(down_weight, 'seq', axis=0, tiled=True)  102 us
    ppermute x4, waiting for transfers between devices, unite_runs(): lax.ppermute(oldest[-1] if oldest else arr_in, group_axis, rack)  99.4 us
    dot_general x9, matrix products, fold_rows(): return jnp.dot(left, portion, preferred_element_type=jnp.float32)  95.2 us
    dot_general x8, matrix products, right_transposed(): lax.dot_general(left, portion, (((1,), (1,)), ((), ())), preferred_elemen...  80.6 us
    unnamed x367, local copies, waits for them, and re-layouts  75.7 us
  transfers between devices with their start and end apart: 16, of which 8 were waited for; matrix products, arithmetic and copies ran while one was open for 35% of the time, Pallas kernels for 0%

profile of v1, /device:TPU:8, one launch (start us, length us, event | category | flops | bytes accessed | tf_op | source)
XLA Modules:
  0.0 2024.1 jit_solution(4371605128149297503)
XLA Ops:
  21.0 227.3 %gather_fusion.1 = bf16[65536,16]{1,0:T(8,128)(2,1)} fusion(bf16[16,961]{0,1:T(8,128)(2,1)S(1)} %copy.147, s32[65536]{0:T(1024)S(1)} %broadcast_clamp_fusion), kind=kCustom, calls=%fused_computation.1 | custom fusion | bytes 4456448 | tf_op jit(solution)/shard_map/jit(_take)/gather | solution.py:195
  248.3 16.8 copy.148
  266.1 38.7 %collective-permute-done.1 = bf16[144,3456]{1,0:T(8,128)(2,1)S(1)} collective-permute-done((bf16[144,3456]{1,0:T(8,128)(2,1)}, bf16[144,3456]{1,0:T(8,128)(2,1)S(1)}, u32[]{:S(2)}, u32[]{:S(2)}) %collective-permute-start.1) | collective-permute-done | bytes 995360 | tf_op jit(solution)/shard_map/ppermute | solution.py:33
  304.8 4.9 convert_bitcast_fusion
  312.1 2.9 collective-permute-start.5
  315.0 44.6 %collective-permute-done.2 = bf16[144,3456]{1,0:T(8,128)(2,1)S(1)} collective-permute-done((bf16[144,3456]{1,0:T(8,128)(2,1)S(1)}, bf16[144,3456]{1,0:T(8,128)(2,1)S(1)}, u32[]{:S(2)}, u32[]{:S(2)}) %collective-permute-start.2) | collective-permute-done | bytes 995360 | tf_op jit(solution)/shard_map/ppermute | solution.py:33
  362.1 3.4 convert_bitcast_fusion.1
  367.9 14.6 collective-permute-done.5
  382.6 16.1 collective-permute-done.3
  412.5 8.2 gather_fusion
  420.7 8.2 convolution_add_fusion
  433.3 9.6 add_convert_fusion.1
  442.9 5.7 copy.143
  448.7 8.3 reshape.913
  457.0 3.9 fusion.219
  474.3 6.4 fusion.214
  480.7 10.0 add_convert_fusion
  490.8 5.7 copy.152
  496.5 8.3 reshape.915
  504.9 5.3 fusion.220
  525.5 4.2 fusion.216
  538.9 11.9 fusion.233
  550.8 8.7 fusion.232
  559.6 102.3 %all-gather.14.cloned.1.call-done = bf16[1152,4608]{1,0:T(8,128)(2,1)} async-done(((bf16[144,4608]{1,0:T(8,128)(2,1)}), bf16[1152,4608]{1,0:T(8,128)(2,1)}) %all-gather.14.cloned.1.call-update) | async-done | bytes 10616848 | tf_op jit(solution)/shard_map/all_gather | solution.py:253
  661.8 11.7 fusion.234
  673.5 24.4 %fusion.11 = (bf16[512,4608]{1,0:T(8,128)(2,1)}, bf16[512,4608]{1,0:T(8,128)(2,1)}, bf16[512,4608]{1,0:T(8,128)(2,1)}, bf16[512,4608]{1,0:T(8,128)(2,1)}) fusion(f32[512,4608]{1,0:T(8,128)} %fusion.232, f32[4608]{0:T(1024)S(1)} %copy-done.98, f32[512,4608]{1,0:T(8,128)} %fusion.233, f32[512,4608]{1,0:T(8,128)} %fusion.234, ...), kind=kOutput, calls=%fused_computation.22 | convolution fusion | flops 5544345600 | bytes 59000832 | tf_op jit(solution)/shard_map/dot_general | solution.py:61
  697.9 12.9 multiply_reduce_fusion.11
  711.5 13.7 multiply_reduce_fusion.9
  725.8 14.4 fusion.213
  740.9 14.3 fusion.212
  755.7 3.8 fusion.71
  767.3 5.4 multiply_reduce_fusion.1
  780.3 3.6 copy.181
  792.6 3.9 reshape.927
  797.2 6.1 multiply_reduce_fusion
  803.8 3.5 multiply_convert_fusion.2
  812.7 5.5 copy.182
  822.0 7.1 convolution_convert_fusion.4
  829.1 5.5 copy.183
  837.7 10.3 multiply_reduce_fusion.10
  848.1 3.1 multiply_reduce_fusion.7
  855.7 10.3 multiply_reduce_fusion.8
  866.1 4.8 multiply_reduce_fusion.4
  872.6 10.9 fusion.4
  883.5 3.5 constant_dynamic-update-slice_fusion.14
  887.0 17.2 fusion.3
  904.2 16.6 fusion.2
  921.0 4.2 multiply_reduce_fusion.6
  927.0 3.5 multiply_reduce_fusion.5
  931.2 8.7 fusion.1
  939.9 749.3 %reduce-scatter.4.cloned.1.call-done = bf16[144,20736]{1,0:T(8,128)(2,1)} async-done(((bf16[1152,20736]{1,0:T(8,128)(2,1)}), bf16[144,20736]{1,0:T(8,128)(2,1)}) %reduce-scatter.4.cloned.1.call-update) | async-done | bytes 5971984 | tf_op jit(solution)/shard_map/reduce_scatter | solution.py:331
  1689.2 61.9 %fusion = bf16[40,20736]{1,0:T(8,128)(2,1)} fusion(bf16[144,20736]{1,0:T(8,128)(2,1)} %reduce-scatter.4.cloned.1.call-done), kind=kCustom, calls=%all-reduce-scatter | all-reduce-scatter fusion | flops 3317761 | bytes 7631360
  1756.6 17.0 concatenate.72
  1773.6 3.1 dynamic-slice_bitcast_fusion
  1776.8 6.8 fusion.32
  1783.6 8.1 bitcast_add_fusion.2
  1791.7 20.2 add.576
  1811.9 33.3 %fusion.185 = f32[31,16,16,16,1]{0,3,2,4,1:T(8,128)} fusion(f32[16,16,16,16,16]{4,3,2,1,0:T(8,128)} %add.576, s32[16,16]{1,0:T(8,128)S(1)} %subtract_add_fusion), kind=kOutput, calls=%fused_computation.267 | convolution fusion | flops 390078208 | bytes 4703232 | tf_op jit(solution)/shard_map/hwxyz,wya->haxz/dot_general | solution.py:170
  1845.2 4.1 fusion.151
  1852.5 4.2 convert_reduce_fusion.1
  1868.5 4.3 convert_reduce_fusion
  1872.8 10.3 reshape.961
  1883.2 5.7 fusion.218
  1895.2 113.8 %all-reduce.5.cloned.1.call-done = (f32[2304]{0:T(1024)}, f32[1152]{0:T(1024)}, f32[4608]{0:T(1024)}, f32[1152]{0:T(1024)}, f32[6912]{0:T(1024)}, /*index=5*/f32[16,961]{1,0:T(8,128)}) async-done(((f32[2304]{0:T(1024)}, f32[1152]{0:T(1024)}, f32[4608]{0:T(1024)}, f32[1152]{0:T(1024)}, f32[6912]{0:T(1024)}, /*index=5*/f32[16,961]{1,0:T(8,128)}), (f32[2304]{0:T(1024)}, f32[1152]{0:T(1024)}, f32[4608]{0:T(1024)}, ...) | async-done | bytes 126032 | tf_op jit(solution)/shard_map/psum | solution.py:344
  (507 shorter events, 160.2 us)
Async XLA Ops:
  7.2 413.5 %all-gather.8.cloned.1.call-start = ((), (), s32[]{:S(2)}) async-start(), calls=%async_computation.1 | async-start | bytes 17915904 | tf_op jit(solution)/shard_map/all_gather | solution.py:198
  7.9 466.4 %all-gather.10.cloned.1.call-start = ((), (), s32[]{:S(2)}) async-start(), calls=%async_computation.2 | async-start | bytes 2985984 | tf_op jit(solution)/shard_map/all_gather | solution.py:243
  8.7 530.3 %all-gather.12.cloned.1.call-start = ((), (), s32[]{:S(2)}) async-start(), calls=%async_computation.3 | async-start | bytes 11943936 | tf_op jit(solution)/shard_map/all_gather | solution.py:249
  9.4 652.4 %all-gather.14.cloned.1.call-start = ((), (), s32[]{:S(2)}) async-start(), calls=%async_computation.4 | async-start | bytes 11943936 | tf_op jit(solution)/shard_map/all_gather | solution.py:253
  10.0 827.6 %all-gather.16.cloned.1.call-start = ((), (), s32[]{:S(2)}) async-start(), calls=%async_computation.5 | async-start | bytes 8957952 | tf_op jit(solution)/shard_map/all_gather | solution.py:294
  10.0 255.1 %collective-permute-start = (bf16[144,3456]{1,0:T(8,128)(2,1)}, bf16[144,3456]{1,0:T(8,128)(2,1)}, u32[]{:S(2)}, u32[]{:S(2)}) collective-permute-start(bf16[144,3456]{1,0:T(8,128)(2,1)} %param.20), channel_id=1, source_target_pairs={{0,1},{1,2},{2,3},{3,4},{4,5},{5,6},{6,7},{7,0},{8,9},{9,10},{10,1... | collective-permute-start | bytes 2985992 | tf_op jit(solution)/shard_map/ppermute | solution.py:33
  11.6 300.5 %collective-permute-start.4 = (bf16[144,3456]{1,0:T(8,128)(2,1)}, bf16[144,3456]{1,0:T(8,128)(2,1)}, u32[]{:S(2)}, u32[]{:S(2)}) collective-permute-start(bf16[144,3456]{1,0:T(8,128)(2,1)} %param.20), channel_id=1, source_target_pairs={{1,0},{2,1},{3,2},{4,3},{5,4},{6,5},{7,6},{0,7},{9,8},{10,9},{11,1... | collective-permute-start | bytes 2985992 | tf_op jit(solution)/shard_map/ppermute | solution.py:35
  13.0 1676.2 %reduce-scatter.4.cloned.1.call-start = ((), (), s32[]{:S(2)}) async-start(), calls=%async_computation.6 | async-start | bytes 53747712 | tf_op jit(solution)/shard_map/reduce_scatter | solution.py:331
  15.7 446.6 %copy-start.122 = (pred[2,256]{1,0:T(4,128)(4,1)}, pred[2,256]{1,0:T(4,128)(4,1)S(1)}, u32[]{:S(2)}) copy-start(pred[2,256]{1,0:T(4,128)(4,1)S(1)} %get-tuple-element.241) | copy-start | bytes 1540
  248.3 17.4 copy-start.127
  248.3 17.5 copy-start.152
  265.2 39.6 %collective-permute-start.1 = (bf16[144,3456]{1,0:T(8,128)(2,1)}, bf16[144,3456]{1,0:T(8,128)(2,1)S(1)}, u32[]{:S(2)}, u32[]{:S(2)}) collective-permute-start(bf16[144,3456]{1,0:T(8,128)(2,1)} %collective-permute-done), channel_id=1, source_target_pairs={{0,1},{1,2},{2,3},{3,4},{4,5},{5,6},{6,7},{7,0},{8,9},{9,10},{10,1... | collective-permute-start | bytes 2985992 | tf_op jit(solution)/shard_map/ppermute | solution.py:33
  265.8 166.5 %copy-start.124 = (f32[3456]{0:T(1024)}, f32[3456]{0:T(1024)S(1)}, u32[]{:S(2)}) copy-start(f32[3456]{0:T(1024)S(1)} %maximum_convert_fusion.2) | copy-start | bytes 41476
  265.8 43.9 %copy-start.134 = (s32[2,256]{1,0:T(2,128)}, s32[2,256]{1,0:T(2,128)S(1)}, u32[]{:S(2)}) copy-start(s32[2,256]{1,0:T(2,128)S(1)} %get-tuple-element.193) | copy-start | bytes 6148
  265.8 196.4 %copy-start.95 = (s32[2,256]{1,0:T(2,128)}, s32[2,256]{1,0:T(2,128)S(1)}, u32[]{:S(2)}) copy-start(s32[2,256]{1,0:T(2,128)S(1)} %get-tuple-element.192) | copy-start | bytes 6148
  304.8 54.8 %collective-permute-start.2 = (bf16[144,3456]{1,0:T(8,128)(2,1)S(1)}, bf16[144,3456]{1,0:T(8,128)(2,1)S(1)}, u32[]{:S(2)}, u32[]{:S(2)}) collective-permute-start(bf16[144,3456]{1,0:T(8,128)(2,1)S(1)} %collective-permute-done.1), channel_id=1, source_target_pairs={{0,1},{1,2},{2,3},{3,4},{4,5},{5,6},{6,7},{7,0},{8,9},{9,10},{10,1... | collective-permute-start | bytes 2985992 | tf_op jit(solution)/shard_map/ppermute | solution.py:33
  309.7 52.4 %copy-start.58 = (bf16[256,256,16]{0,1,2:T(8,128)(2,1)S(1)}, bf16[256,256,16]{0,1,2:T(8,128)(2,1)}, u32[]{:S(2)}) copy-start(bf16[256,256,16]{0,1,2:T(8,128)(2,1)} %copy.148) | copy-start | bytes 6291460
  312.1 70.3 %collective-permute-start.5 = (bf16[144,3456]{1,0:T(8,128)(2,1)}, bf16[144,3456]{1,0:T(8,128)(2,1)S(1)}, u32[]{:S(2)}, u32[]{:S(2)}) collective-permute-start(bf16[144,3456]{1,0:T(8,128)(2,1)} %collective-permute-done.4), channel_id=1, source_target_pairs={{1,0},{2,1},{3,2},{4,3},{5,4},{6,5},{7,6},{0,7},{9,8},{10,9},{11,1... | collective-permute-start | bytes 2985992 | tf_op jit(solution)/shard_map/ppermute | solution.py:35
  359.6 39.2 %collective-permute-start.3 = (bf16[144,3456]{1,0:T(8,128)(2,1)S(1)}, bf16[144,3456]{1,0:T(8,128)(2,1)S(1)}, u32[]{:S(2)}, u32[]{:S(2)}) collective-permute-start(bf16[144,3456]{1,0:T(8,128)(2,1)S(1)} %collective-permute-done.2), channel_id=1, source_target_pairs={{0,1},{1,2},{2,3},{3,4},{4,5},{5,6},{6,7},{7,0},{8,9},{9,10},{10,1... | collective-permute-start | bytes 2985992 | tf_op jit(solution)/shard_map/ppermute | solution.py:33
  382.5 29.0 %collective-permute-start.6 = (bf16[144,3456]{1,0:T(8,128)(2,1)S(1)}, bf16[144,3456]{1,0:T(8,128)(2,1)S(1)}, u32[]{:S(2)}, u32[]{:S(2)}) collective-permute-start(bf16[144,3456]{1,0:T(8,128)(2,1)S(1)} %collective-permute-done.5), channel_id=1, source_target_pairs={{1,0},{2,1},{3,2},{4,3},{5,4},{6,5},{7,6},{0,7},{9,8},{10,9},{11,1... | collective-permute-start | bytes 2985992 | tf_op jit(solution)/shard_map/ppermute | solution.py:35
  429.7 13.3 copy-start.73
  480.7 10.1 copy-start.61
  510.1 9.6 copy-start.36
  513.5 19.8 copy-start.99
  533.3 207.5 %copy-start.71 = (f32[2,1152]{1,0:T(2,128)}, f32[2,1152]{1,0:T(2,128)S(1)}, u32[]{:S(2)}) copy-start(f32[2,1152]{1,0:T(2,128)S(1)} %get-tuple-element.239) | copy-start | bytes 27652
  533.4 192.4 %copy-start.78 = (f32[2,1152]{1,0:T(2,128)}, f32[2,1152]{1,0:T(2,128)S(1)}, u32[]{:S(2)}) copy-start(f32[2,1152]{1,0:T(2,128)S(1)} %get-tuple-element.235) | copy-start | bytes 27652
  538.9 11.9 copy-start.63
  538.9 11.9 copy-start.155
  661.8 11.7 copy-start.5
  661.8 11.7 copy-start.98
  711.5 14.3 copy-start.106
  711.5 14.3 copy-start.85
  711.5 14.3 copy-start.102
  711.5 14.3 copy-start.147
  725.8 15.0 copy-start.104
  725.8 15.0 copy-start.100
  725.8 15.0 copy-start.149
  740.9 14.9 copy-start.68
  837.6 10.4 copy-start.120
  837.6 10.4 copy-start.139
  837.6 10.4 copy-start.1
  837.6 10.4 copy-start.12
  837.6 10.4 copy-start.14
  837.7 10.4 copy-start.33
  837.7 10.4 copy-start.74
  837.7 10.4 copy-start.110
  855.7 10.3 copy-start.138
  855.7 10.4 copy-start.11
  855.7 10.4 copy-start.13
  855.7 10.4 copy-start.70
  855.7 10.4 copy-start.111
  872.6 10.9 copy-start.16
  887.0 17.2 copy-start.51
  904.2 16.7 copy-start.72
  904.2 16.7 copy-start.121
  904.2 16.7 copy-start.123
  904.2 16.7 copy-start.133
  904.2 16.7 copy-start.136
  939.9 815.5 %copy-start.154 = (u32[32]{0:T(128)S(1)}, u32[32]{0:T(128)}, u32[]{:S(2)}) copy-start(u32[32]{0:T(128)} %constant.216) | copy-start | bytes 388
  939.9 932.9 %all-gather.18.cloned.1.call-start = ((), (), s32[]{:S(2)}) async-start(), calls=%async_computation.7 | async-start | bytes 8294400 | tf_op jit(solution)/shard_map/all_gather | solution.py:335
  1753.2 3.4 collective-permute-start.7
  1776.8 232.3 %all-reduce.5.cloned.1.call-start = ((), (), s32[]{:S(2)}) async-start(), calls=%async_computation.8 | async-start | bytes 286720 | tf_op jit(solution)/shard_map/psum | solution.py:344
  1852.5 8.5 copy-start.75
  1883.2 8.5 copy-start.4
  (114 other events, 424.5 us)
Sparse Core Ops, SparseCore 0:
  10.2 234.5 all-gather.7
  247.0 70.3 all-gather.9
  319.6 189.5 all-gather.11
  511.2 150.6 all-gather.13
  663.9 117.7 all-gather.15
  940.0 749.1 reduce-scatter.3
  1776.9 57.1 all-gather.17
  1872.9 136.0 all-reduce.4
